TPU v7x, 256 devices: a whole 4x4x8 slice. The times are simulated.
256 devices in a mesh: blk: 32 (over z_lo, x, core), grp: 8 (over z_hi, y).
Axes of the slice: x: 4, y: 4, z: 8 (z_hi: 2, z_lo: 4; z = z_hi * 4 + z_lo), core: 2. Of those that a mesh axis runs over, the one named last changes fastest.
Arguments:
- lambda_init: float32 [131072, 256], P('blk'), may hold values from 0.1 to 200
- gamma_init: float32 [32768, 256], P(('blk', 'grp')), may hold values from 0.5 to 20
- dmr_table: float32 [1024, 256], replicated, may hold values from -3 to 3
- features: int32 [32768, 4], P(('blk', 'grp')), may hold values from 0 to 1023
- counts: int32 [256, 4, 6, 128, 128], P(('blk', 'grp')), may hold values from 0 to 3
- tile_cols: int32 [256, 4, 6], P(('blk', 'grp')), may hold values from 0 to 31, as said below
- live_slots: int32 [256, 4], P(('blk', 'grp')), may hold values from 1 to 6, as said below
Outputs:
- gamma_out: float32 [32768, 256], P(('blk', 'grp'))
- lambda_out: float32 [131072, 256], P(('blk', 'grp'))
Inputs may be any that keep to these rules, and one draw needn't show every extreme that they name: `tile_cols`: within one row tile and substep the 6 column tiles are distinct. Slots 0 to live_slots - 1 of a row tile and substep are in use, the others are padding; row tile 0 uses all 6 slots in substep 0.
All inputs are finite; a program needn't handle non-finite values.
Results may differ from a plain program's by a relative error of at most 0.009.
Values sent between devices are 32-bit elements; how exact they have to be, the bound alone decides.
A program may use at most 128 MiB of HBM per device.

v0:
```python
import jax
import jax.numpy as jnp
from jax import lax
from jax.sharding import PartitionSpec as P

STRATA = 4
LOCAL = 3
pass_bits = (0, 1, 0)
step_weight = 0.5
word_prior = 0.05


def partner(value, axis, bit):
    mask = 2**bit
    pairs = [(source, source ^ mask) for source in range(lax.axis_size(axis))]
    return lax.ppermute(value, axis, pairs)


def expected_theta(doc_gamma):
    return jnp.exp(
        lax.digamma(doc_gamma) - lax.digamma(jnp.sum(doc_gamma, axis=1, keepdims=True))
    ).astype(jnp.bfloat16)


def update_padded(doc_gamma, doc_alpha, beta_exp, tile_counts, column_ids, live_count):
    rows, slots = column_ids.shape
    tile = tile_counts.shape[-1]
    topics = beta_exp.shape[1]
    columns = beta_exp.shape[0] // tile
    word_tiles = beta_exp.reshape(columns, tile, topics)[column_ids]
    active = jnp.arange(slots)[None, :] < live_count[:, None]
    tile_weight = jnp.where(active[:, :, None, None], tile_counts, 0).astype(jnp.float32)

    def ratio_of(theta_exp):
        theta_rows = theta_exp.reshape(rows, tile, topics)
        denom_tiles = jnp.einsum(
            "rdk,rswk->rsdw", theta_rows, word_tiles, preferred_element_type=jnp.float32
        )
        return (theta_rows, (tile_weight / denom_tiles).astype(jnp.bfloat16))

    for repeat in range(LOCAL):
        theta_exp = expected_theta(doc_gamma)
        theta_rows, count_ratio = ratio_of(theta_exp)
        contrib = jnp.einsum(
            "rsdw,rswk->rdk", count_ratio, word_tiles, preferred_element_type=jnp.float32
        )
        doc_gamma = doc_alpha + theta_exp.astype(jnp.float32) * contrib.reshape(doc_gamma.shape)
    theta_exp = expected_theta(doc_gamma)
    theta_rows, count_ratio = ratio_of(theta_exp)
    stat_tiles = jnp.einsum(
        "rsdw,rdk->rswk", count_ratio, theta_rows, preferred_element_type=jnp.float32
    )
    selector = (column_ids.reshape(-1)[None, :] == jnp.arange(columns)[:, None]).astype(jnp.float32)
    accumulated = jnp.dot(
        selector,
        stat_tiles.reshape(rows * slots, tile * topics),
        precision=lax.Precision.HIGHEST,
        preferred_element_type=jnp.float32,
    )
    partial_value = (beta_exp.astype(jnp.float32) * accumulated.reshape(beta_exp.shape)).astype(
        jnp.bfloat16
    )
    return (doc_gamma, partial_value)


def on_device(lambda_init, gamma_init, dmr_table, features, counts, tile_cols, live_slots):
    groups = lax.axis_size("grp")
    doc_alpha = jnp.exp(jnp.sum(jnp.take(dmr_table, features, axis=0), axis=1))
    topic_panel = lambda_init
    doc_gamma = gamma_init
    ahead = [(counts[:, step], tile_cols[:, step], live_slots[:, step]) for step in range(STRATA)]
    for substep in range(STRATA):
        topic_totals = lax.psum(jnp.sum(topic_panel, axis=0), "blk")
        beta_exp = jnp.exp(lax.digamma(topic_panel) - lax.digamma(topic_totals)[None, :]).astype(
            jnp.bfloat16
        )
        tile_counts, column_ids, live_count = ahead[substep]
        doc_gamma, partial_value = update_padded(
            doc_gamma, doc_alpha, beta_exp, tile_counts, column_ids, live_count
        )
        partial_wide = partial_value.astype(jnp.float32)
        topic_panel = (1.0 - step_weight) * topic_panel + step_weight * (
            word_prior + groups * partial_wide
        )
        if substep + 1 < STRATA:
            topic_panel = partner(topic_panel, "blk", pass_bits[substep])
    returned = partner(topic_panel, "blk", 1)
    lambda_out = lax.psum_scatter(returned, "grp", scatter_dimension=0, tiled=True) / groups
    return (doc_gamma, lambda_out)


def solution(mesh):
    placed = (
        P("blk", None),
        P(("blk", "grp"), None),
        P(),
        P(("blk", "grp"), None),
        P(("blk", "grp"), None, None, None, None),
        P(("blk", "grp"), None, None),
        P(("blk", "grp"), None),
    )
    return jax.shard_map(
        on_device,
        mesh=mesh,
        in_specs=placed,
        out_specs=(P(("blk", "grp"), None), P(("blk", "grp"), None)),
        check_vma=False,
    )
```

profile of v0, /device:TPU:2, one launch (start us, length us, event | category | flops | bytes accessed | tf_op | source)
XLA Modules:
  0.0 971.4 jit_solution(11349944712622576817)
XLA Ops:
  17.0 68.1 %psum.28 = f32[256]{0:T(256)S(1)} all-reduce(f32[256]{0:T(256)S(1)} %reduce_sum.176), channel_id=1, replica_groups=mesh['blk'=32,'grp'=8] {'blk'}, use_global_device_ids=true, to_apply=%region_3.4 | all-reduce | flops 256 | bytes 2048 | tf_op jit(solution)/shard_map/psum | solution.py:73
  85.2 31.2 %fusion.4 = bf16[4096,256]{1,0:T(8,128)(2,1)} fusion(f32[4096,256]{1,0:T(8,128)} %param.7, f32[256]{0:T(256)S(1)} %compare_select_fusion.20), kind=kLoop, calls=%fused_computation.17 | loop fusion | flops 80740352 | bytes 6292480 | tf_op jit(solution)/shard_map/convert_element_type | solution.py:74
  135.2 4.9 reshape.2574
  140.1 33.2 %add_multiply_fusion.3 = f32[4096,256]{1,0:T(8,128)} fusion(f32[4096,256]{1,0:T(8,128)} %param.7, f32[4096,256]{1,0:T(8,128)} %reshape.2574, f32[256]{0:T(256)S(1)} %copy-done.7), kind=kLoop, calls=%fused_computation.39 | loop fusion | flops 89128960 | bytes 12583936 | tf_op jit(solution)/shard_map/add | solution.py:82
  174.3 6.7 collective-permute-done
  183.7 67.9 %psum.29 = f32[256]{0:T(256)S(1)} all-reduce(f32[256]{0:T(256)S(1)} %reduce_sum.180), channel_id=1, replica_groups=mesh['blk'=32,'grp'=8] {'blk'}, use_global_device_ids=true, to_apply=%region_8.9 | all-reduce | flops 256 | bytes 2048 | tf_op jit(solution)/shard_map/psum | solution.py:73
  251.6 31.1 %fusion.9 = bf16[4096,256]{1,0:T(8,128)(2,1)} fusion(f32[4096,256]{1,0:T(8,128)} %collective-permute-done, f32[256]{0:T(256)S(1)} %compare_select_fusion.16), kind=kLoop, calls=%fused_computation.22 | loop fusion | flops 80740352 | bytes 6292480 | tf_op jit(solution)/shard_map/convert_element_type | solution.py:74
  292.9 3.7 fusion.797
  296.6 4.9 reshape.2582
  301.5 33.2 %add_multiply_fusion.2 = f32[4096,256]{1,0:T(8,128)} fusion(f32[4096,256]{1,0:T(8,128)} %collective-permute-done, f32[4096,256]{1,0:T(8,128)} %reshape.2582, f32[256]{0:T(256)S(1)} %compare_select_fusion.16), kind=kLoop, calls=%fused_computation.37 | loop fusion | flops 89128960 | bytes 12583936 | tf_op jit(solution)/shard_map/add | solution.py:82
  334.7 6.4 collective-permute-start.1
  342.0 90.0 %collective-permute-done.1 = f32[4096,256]{1,0:T(8,128)} collective-permute-done((f32[4096,256]{1,0:T(8,128)}, f32[4096,256]{1,0:T(8,128)}, u32[]{:S(2)}, u32[]{:S(2)}) %collective-permute-start.1) | collective-permute-done | bytes 4194336 | tf_op jit(solution)/shard_map/ppermute | solution.py:16
  434.7 62.9 %psum.30 = f32[256]{0:T(256)S(1)} all-reduce(f32[256]{0:T(256)S(1)} %reduce_sum.184), channel_id=1, replica_groups=mesh['blk'=32,'grp'=8] {'blk'}, use_global_device_ids=true, to_apply=%region_13.14 | all-reduce | flops 256 | bytes 2048 | tf_op jit(solution)/shard_map/psum | solution.py:73
  497.7 31.1 %fusion.14 = bf16[4096,256]{1,0:T(8,128)(2,1)} fusion(f32[4096,256]{1,0:T(8,128)} %collective-permute-done.1, f32[256]{0:T(256)S(1)} %compare_select_fusion.12), kind=kLoop, calls=%fused_computation.27 | loop fusion | flops 80740352 | bytes 6292480 | tf_op jit(solution)/shard_map/convert_element_type | solution.py:74
  542.1 4.9 reshape.2590
  546.9 33.2 %add_multiply_fusion.1 = f32[4096,256]{1,0:T(8,128)} fusion(f32[4096,256]{1,0:T(8,128)} %collective-permute-done.1, f32[4096,256]{1,0:T(8,128)} %reshape.2590, f32[256]{0:T(256)S(1)} %compare_select_fusion.12), kind=kLoop, calls=%fused_computation.35 | loop fusion | flops 89128960 | bytes 12583936 | tf_op jit(solution)/shard_map/add | solution.py:82
  581.3 6.7 collective-permute-done.2
  590.7 67.5 %psum.31 = f32[256]{0:T(256)S(1)} all-reduce(f32[256]{0:T(256)S(1)} %reduce_sum.188), channel_id=1, replica_groups=mesh['blk'=32,'grp'=8] {'blk'}, use_global_device_ids=true, to_apply=%region_18.19 | all-reduce | flops 256 | bytes 2048 | tf_op jit(solution)/shard_map/psum | solution.py:73
  658.2 31.0 %fusion.19 = bf16[4096,256]{1,0:T(8,128)(2,1)} fusion(f32[4096,256]{1,0:T(8,128)} %collective-permute-done.2, f32[256]{0:T(256)S(1)} %compare_select_fusion.8), kind=kLoop, calls=%fused_computation.32 | loop fusion | flops 80740352 | bytes 6292480 | tf_op jit(solution)/shard_map/convert_element_type | solution.py:74
  703.4 4.9 reshape.2598
  708.3 31.3 %add_multiply_fusion = f32[4096,256]{1,0:T(8,128)S(1)} fusion(f32[4096,256]{1,0:T(8,128)} %collective-permute-done.2, f32[4096,256]{1,0:T(8,128)} %reshape.2598, f32[256]{0:T(256)S(1)} %compare_select_fusion.8), kind=kLoop, calls=%fused_computation.33 | loop fusion | flops 89128960 | bytes 12583936 | tf_op jit(solution)/shard_map/add | solution.py:82
  739.6 6.3 collective-permute-start.3
  745.9 90.6 %collective-permute-done.3 = f32[4096,256]{1,0:T(8,128)} collective-permute-done((f32[4096,256]{1,0:T(8,128)S(1)}, f32[4096,256]{1,0:T(8,128)}, u32[]{:S(2)}, u32[]{:S(2)}) %collective-permute-start.3) | collective-permute-done | bytes 4194336 | tf_op jit(solution)/shard_map/ppermute | solution.py:16
  836.5 126.0 %reduce-scatter.2.cloned.1.call-done = f32[512,256]{1,0:T(8,128)} async-done(((f32[4096,256]{1,0:T(8,128)}), f32[512,256]{1,0:T(8,128)}) %reduce-scatter.2.cloned.1.call-update) | async-done | bytes 524304 | tf_op jit(solution)/shard_map/reduce_scatter | solution.py:88
  (122 shorter events, 79.0 us)
Async XLA Ops:
  7.2 4.6 copy-start
  7.2 955.3 %reduce-scatter.2.cloned.1.call-start = ((), (), s32[]{:S(2)}) async-start(), calls=%async_computation.1 | async-start | bytes 4718592 | tf_op jit(solution)/shard_map/reduce_scatter | solution.py:88
  17.0 99.4 %copy-start.2 = (s32[1,4,6,128,128]{4,3,2,1,0:T(8,128)S(1)}, s32[1,4,6,128,128]{4,3,2,1,0:T(8,128)}, u32[]{:S(2)}) copy-start(s32[1,4,6,128,128]{4,3,2,1,0:T(8,128)} %param.11) | copy-start | bytes 4718596
  85.2 32.1 %copy-start.6 = (f32[256]{0:T(256)}, f32[256]{0:T(256)S(1)}, u32[]{:S(2)}) copy-start(f32[256]{0:T(256)S(1)} %compare_select_fusion.20) | copy-start | bytes 3076
  85.2 32.3 %copy-start.5 = (s32[1,4]{1,0:T(1,128)S(1)}, s32[1,4]{1,0:T(1,128)}, u32[]{:S(2)}) copy-start(s32[1,4]{1,0:T(1,128)} %param.13) | copy-start | bytes 52
  85.2 33.7 %copy-start.4 = (f32[128,256]{1,0:T(8,128)S(1)}, f32[128,256]{1,0:T(8,128)}, u32[]{:S(2)}) copy-start(f32[128,256]{1,0:T(8,128)} %param.8) | copy-start | bytes 393220
  126.5 4.9 copy-start.14
  129.9 0.6 copy-start.18
  135.2 4.9 copy-start.7
  140.1 33.3 %copy-start.3 = (s32[1,1,6,128,128]{4,3,2,1,0:T(8,128)S(1)}, s32[1,1,6,128,128]{4,3,2,1,0:T(8,128)}, u32[]{:S(2)}) copy-start(s32[1,1,6,128,128]{4,3,2,1,0:T(8,128)} %get-tuple-element.4) | copy-start | bytes 1179652
  140.1 34.2 %copy-start.10 = (s32[6]{0:T(128)S(1)}, s32[6]{0:T(128)}, u32[]{:S(2)}) copy-start(s32[6]{0:T(128)} %get-tuple-element.11) | copy-start | bytes 76
  173.4 7.6 collective-permute-start
  251.6 33.2 %copy-start.19 = (bf16[128,256]{1,0:T(8,128)(2,1)S(1)}, bf16[128,256]{1,0:T(8,128)(2,1)}, u32[]{:S(2)}) copy-start(bf16[128,256]{1,0:T(8,128)(2,1)} %copy-done.18) | copy-start | bytes 196612
  287.9 5.0 copy-start.13
  301.5 40.4 %copy-start.9 = (s32[6]{0:T(128)S(1)}, s32[6]{0:T(128)}, u32[]{:S(2)}) copy-start(s32[6]{0:T(128)} %get-tuple-element.13) | copy-start | bytes 76
  334.7 97.2 %collective-permute-start.1 = (f32[4096,256]{1,0:T(8,128)}, f32[4096,256]{1,0:T(8,128)}, u32[]{:S(2)}, u32[]{:S(2)}) collective-permute-start(f32[4096,256]{1,0:T(8,128)} %add_multiply_fusion.2), channel_id=1, source_target_pairs={{0,16},{8,24},{16,0},{24,8},{32,48},{40,56},{48,32},{56,40},{64,80... | collective-permute-start | bytes 12582920 | tf_op jit(solution)/shard_map/ppermute | solution.py:16
  497.7 33.2 %copy-start.17 = (bf16[128,256]{1,0:T(8,128)(2,1)S(1)}, bf16[128,256]{1,0:T(8,128)(2,1)}, u32[]{:S(2)}) copy-start(bf16[128,256]{1,0:T(8,128)(2,1)} %copy-done.16) | copy-start | bytes 196612
  534.0 4.3 copy-start.12
  546.9 34.3 %copy-start.8 = (s32[6]{0:T(128)S(1)}, s32[6]{0:T(128)}, u32[]{:S(2)}) copy-start(s32[6]{0:T(128)} %get-tuple-element.10) | copy-start | bytes 76
  580.1 7.8 collective-permute-start.2
  696.8 2.3 copy-start.15
  696.9 2.7 copy-start.11
  708.3 256.0 %copy-start.1 = (f32[1024,256]{1,0:T(8,128)S(1)}, f32[1024,256]{1,0:T(8,128)}, u32[]{:S(2)}) copy-start(f32[1024,256]{1,0:T(8,128)} %param.9) | copy-start | bytes 3145732
  739.6 96.8 %collective-permute-start.3 = (f32[4096,256]{1,0:T(8,128)S(1)}, f32[4096,256]{1,0:T(8,128)}, u32[]{:S(2)}, u32[]{:S(2)}) collective-permute-start(f32[4096,256]{1,0:T(8,128)S(1)} %add_multiply_fusion), channel_id=1, source_target_pairs={{0,16},{8,24},{16,0},{24,8},{32,48},{40,56},{48,32},{56,40},{64,80... | collective-permute-start | bytes 12582920 | tf_op jit(solution)/shard_map/ppermute | solution.py:16
  (1 other events, 0.6 us)
Sparse Core Ops, SparseCore 0:
  836.6 125.7 reduce-scatter.1
where the time goes:
time: 976 us; the launch traced here: 971 us
  waiting for transfers between devices  320 us (33%)
  other arithmetic  278 us (28%)
  blocking collectives  266 us (27%)
  matrix products  41.4 us (4%)
  local copies, waits for them, and re-layouts  37.3 us (4%)
  between operations  14.9 us (2%)
  starting transfers between devices  13.1 us (1%)
    psum x4, blocking collectives, on_device(): topic_totals = lax.psum(jnp.sum(topic_panel, axis=0), 'blk')  266 us
    ppermute x4, waiting for transfers between devices, partner(): return lax.ppermute(value, axis, pairs)  194 us
    add x4, other arithmetic, on_device(): (1.0 - step_weight) * topic_panel  131 us
    reduce_scatter x1, waiting for transfers between devices, on_device(): lax.psum_scatter(returned, 'grp', scatter_dimension=0, tiled=True) / groups  126 us
    convert_element_type x4, other arithmetic, on_device(): jnp.exp(lax.digamma(topic_panel) - lax.digamma(topic_totals)[None, :])  124 us
    dot_general x12, matrix products, update_padded(): jnp.einsum('rsdw,rswk->rdk', count_ratio, word_tiles, preferred_element_t...  22.8 us
    reshape x4, local copies, waits for them, and re-layouts, update_padded(): accumulated.reshape(beta_exp.shape)  19.6 us
  transfers between devices with their start and end apart: 5, of which 5 were waited for; matrix products, arithmetic and copies ran while one was open for 0% of the time, Pallas kernels for 0%

commit v1 on v0

--- a/solution.py
+++ b/solution.py
@@ -8,6 +8,12 @@
 pass_bits = (0, 1, 0)
 step_weight = 0.5
 word_prior = 0.05
+
+
+def gather_and_add(shard, axis):
+    parts = lax.all_gather(shard, axis, axis=0, tiled=False)
+    total = parts.sum(axis=0)
+    return total
 
 
 def partner(value, axis, bit):
@@ -70,7 +76,7 @@
     doc_gamma = gamma_init
     ahead = [(counts[:, step], tile_cols[:, step], live_slots[:, step]) for step in range(STRATA)]
     for substep in range(STRATA):
-        topic_totals = lax.psum(jnp.sum(topic_panel, axis=0), "blk")
+        topic_totals = gather_and_add(jnp.sum(topic_panel, axis=0), "blk")
         beta_exp = jnp.exp(lax.digamma(topic_panel) - lax.digamma(topic_totals)[None, :]).astype(
             jnp.bfloat16
         )

time: 976 us -> 862 us (0.88)
  blocking collectives: 266 us -> 160 us
  starting transfers between devices: 13.1 us -> 1.88 us
    psum x4 -> x0, blocking collectives: 266 us -> none  [on_device(): topic_totals = lax.psum(jnp.sum(topic_panel, axis=0), 'blk')]
    all_gather x0 -> x4, blocking collectives: none -> 160 us  [gather_and_add(): parts = lax.all_gather(shard, axis, axis=0, tiled=False)]
    ppermute x4, starting transfers between devices: 13.1 us -> 1.84 us  [partner(): return lax.ppermute(value, axis, pairs)]
where the time goes in v1:
time: 862 us; the launch traced here: 857 us
  waiting for transfers between devices  323 us (37%)
  other arithmetic  279 us (32%)
  blocking collectives  160 us (19%)
  matrix products  41.4 us (5%)
  local copies, waits for them, and re-layouts  37.3 us (4%)
  between operations  14.9 us (2%)
    ppermute x4, waiting for transfers between devices, partner(): return lax.ppermute(value, axis, pairs)  197 us
    all_gather x4, blocking collectives, gather_and_add(): parts = lax.all_gather(shard, axis, axis=0, tiled=False)  160 us
    add x4, other arithmetic, on_device(): (1.0 - step_weight) * topic_panel  131 us
    reduce_scatter x1, waiting for transfers between devices, on_device(): lax.psum_scatter(returned, 'grp', scatter_dimension=0, tiled=True) / groups  125 us
    convert_element_type x4, other arithmetic, on_device(): jnp.exp(lax.digamma(topic_panel) - lax.digamma(topic_totals)[None, :])  125 us
    dot_general x12, matrix products, update_padded(): jnp.einsum('rsdw,rswk->rdk', count_ratio, word_tiles, preferred_element_t...  22.8 us
    reshape x4, local copies, waits for them, and re-layouts, update_padded(): accumulated.reshape(beta_exp.shape)  19.6 us
  transfers between devices with their start and end apart: 5, of which 5 were waited for; matrix products, arithmetic and copies ran while one was open for 0% of the time, Pallas kernels for 0%

profile of v1, /device:TPU:2, one launch (start us, length us, event | category | flops | bytes accessed | tf_op | source)
XLA Modules:
  0.0 857.2 jit_solution(2237652085848487461)
XLA Ops:
  17.0 40.0 %all-gather.4 = f32[32,1,256]{2,1,0:T(1,128)S(1)} all-gather(f32[1,1,256]{2,1,0:T(1,128)S(1)} %bitcast.637), channel_id=2, replica_groups=mesh['blk'=32,'grp'=8] {'blk'}, dimensions={0}, use_global_device_ids=true | all-gather | bytes 33792 | tf_op jit(solution)/shard_map/all_gather | solution.py:14
  57.1 31.2 %fusion.4 = bf16[4096,256]{1,0:T(8,128)(2,1)} fusion(f32[4096,256]{1,0:T(8,128)} %param.7, f32[256]{0:T(256)S(1)} %compare_select_fusion.20), kind=kLoop, calls=%fused_computation.17 | loop fusion | flops 80740352 | bytes 6292480 | tf_op jit(solution)/shard_map/convert_element_type | solution.py:80
  107.1 4.9 reshape.2890
  112.1 33.2 %add_multiply_fusion.3 = f32[4096,256]{1,0:T(8,128)} fusion(f32[4096,256]{1,0:T(8,128)} %param.7, f32[4096,256]{1,0:T(8,128)} %reshape.2890, f32[256]{0:T(256)S(1)} %copy-done.7), kind=kLoop, calls=%fused_computation.39 | loop fusion | flops 89128960 | bytes 12583936 | tf_op jit(solution)/shard_map/add | solution.py:88
  146.5 6.4 collective-permute-done
  155.6 42.6 %all-gather.5 = f32[32,1,256]{2,1,0:T(1,128)S(1)} all-gather(f32[1,1,256]{2,1,0:T(1,128)S(1)} %bitcast.638), channel_id=3, replica_groups=mesh['blk'=32,'grp'=8] {'blk'}, dimensions={0}, use_global_device_ids=true | all-gather | bytes 33792 | tf_op jit(solution)/shard_map/all_gather | solution.py:14
  198.4 31.4 %fusion.9 = bf16[4096,256]{1,0:T(8,128)(2,1)} fusion(f32[4096,256]{1,0:T(8,128)} %collective-permute-done, f32[256]{0:T(256)S(1)} %compare_select_fusion.16), kind=kLoop, calls=%fused_computation.22 | loop fusion | flops 80740352 | bytes 6292480 | tf_op jit(solution)/shard_map/convert_element_type | solution.py:80
  240.0 3.7 fusion.797
  243.8 4.9 reshape.2898
  248.7 33.2 %add_multiply_fusion.2 = f32[4096,256]{1,0:T(8,128)} fusion(f32[4096,256]{1,0:T(8,128)} %collective-permute-done, f32[4096,256]{1,0:T(8,128)} %reshape.2898, f32[256]{0:T(256)S(1)} %compare_select_fusion.16), kind=kLoop, calls=%fused_computation.37 | loop fusion | flops 89128960 | bytes 12583936 | tf_op jit(solution)/shard_map/add | solution.py:88
  283.1 92.0 %collective-permute-done.1 = f32[4096,256]{1,0:T(8,128)} collective-permute-done((f32[4096,256]{1,0:T(8,128)}, f32[4096,256]{1,0:T(8,128)}, u32[]{:S(2)}, u32[]{:S(2)}) %collective-permute-start.1) | collective-permute-done | bytes 4194336 | tf_op jit(solution)/shard_map/ppermute | solution.py:22
  377.8 38.1 %all-gather.6 = f32[32,1,256]{2,1,0:T(1,128)S(1)} all-gather(f32[1,1,256]{2,1,0:T(1,128)S(1)} %bitcast.639), channel_id=4, replica_groups=mesh['blk'=32,'grp'=8] {'blk'}, dimensions={0}, use_global_device_ids=true | all-gather | bytes 33792 | tf_op jit(solution)/shard_map/all_gather | solution.py:14
  416.0 31.1 %fusion.14 = bf16[4096,256]{1,0:T(8,128)(2,1)} fusion(f32[4096,256]{1,0:T(8,128)} %collective-permute-done.1, f32[256]{0:T(256)S(1)} %compare_select_fusion.12), kind=kLoop, calls=%fused_computation.27 | loop fusion | flops 80740352 | bytes 6292480 | tf_op jit(solution)/shard_map/convert_element_type | solution.py:80
  456.6 3.7 fusion.798
  460.4 4.9 reshape.2906
  465.2 33.2 %add_multiply_fusion.1 = f32[4096,256]{1,0:T(8,128)} fusion(f32[4096,256]{1,0:T(8,128)} %collective-permute-done.1, f32[4096,256]{1,0:T(8,128)} %reshape.2906, f32[256]{0:T(256)S(1)} %compare_select_fusion.12), kind=kLoop, calls=%fused_computation.35 | loop fusion | flops 89128960 | bytes 12583936 | tf_op jit(solution)/shard_map/add | solution.py:88
  499.9 6.4 collective-permute-done.2
  509.0 39.3 %all-gather.7 = f32[32,1,256]{2,1,0:T(1,128)S(1)} all-gather(f32[1,1,256]{2,1,0:T(1,128)S(1)} %bitcast.640), channel_id=5, replica_groups=mesh['blk'=32,'grp'=8] {'blk'}, dimensions={0}, use_global_device_ids=true | all-gather | bytes 33792 | tf_op jit(solution)/shard_map/all_gather | solution.py:14
  548.4 31.0 %fusion.19 = bf16[4096,256]{1,0:T(8,128)(2,1)} fusion(f32[4096,256]{1,0:T(8,128)} %collective-permute-done.2, f32[256]{0:T(256)S(1)} %compare_select_fusion.8), kind=kLoop, calls=%fused_computation.32 | loop fusion | flops 80740352 | bytes 6292480 | tf_op jit(solution)/shard_map/convert_element_type | solution.py:80
  589.8 3.7 fusion.799
  593.5 4.9 reshape.2914
  598.4 31.3 %add_multiply_fusion = f32[4096,256]{1,0:T(8,128)S(1)} fusion(f32[4096,256]{1,0:T(8,128)} %collective-permute-done.2, f32[4096,256]{1,0:T(8,128)} %reshape.2914, f32[256]{0:T(256)S(1)} %compare_select_fusion.8), kind=kLoop, calls=%fused_computation.33 | loop fusion | flops 89128960 | bytes 12583936 | tf_op jit(solution)/shard_map/add | solution.py:88
  630.2 92.6 %collective-permute-done.3 = f32[4096,256]{1,0:T(8,128)} collective-permute-done((f32[4096,256]{1,0:T(8,128)S(1)}, f32[4096,256]{1,0:T(8,128)}, u32[]{:S(2)}, u32[]{:S(2)}) %collective-permute-start.3) | collective-permute-done | bytes 4194336 | tf_op jit(solution)/shard_map/ppermute | solution.py:22
  722.8 125.4 %reduce-scatter.2.cloned.1.call-done = f32[512,256]{1,0:T(8,128)} async-done(((f32[4096,256]{1,0:T(8,128)}), f32[512,256]{1,0:T(8,128)}) %reduce-scatter.2.cloned.1.call-update) | async-done | bytes 524304 | tf_op jit(solution)/shard_map/reduce_scatter | solution.py:94
  (126 shorter events, 73.2 us)
Async XLA Ops:
  7.2 4.6 copy-start
  7.2 841.0 %reduce-scatter.2.cloned.1.call-start = ((), (), s32[]{:S(2)}) async-start(), calls=%async_computation.1 | async-start | bytes 4718592 | tf_op jit(solution)/shard_map/reduce_scatter | solution.py:94
  17.0 71.4 %copy-start.2 = (s32[1,4,6,128,128]{4,3,2,1,0:T(8,128)S(1)}, s32[1,4,6,128,128]{4,3,2,1,0:T(8,128)}, u32[]{:S(2)}) copy-start(s32[1,4,6,128,128]{4,3,2,1,0:T(8,128)} %param.11) | copy-start | bytes 4718596
  57.1 32.1 %copy-start.6 = (f32[256]{0:T(256)}, f32[256]{0:T(256)S(1)}, u32[]{:S(2)}) copy-start(f32[256]{0:T(256)S(1)} %compare_select_fusion.20) | copy-start | bytes 3076
  57.1 32.3 %copy-start.5 = (s32[1,4]{1,0:T(1,128)S(1)}, s32[1,4]{1,0:T(1,128)}, u32[]{:S(2)}) copy-start(s32[1,4]{1,0:T(1,128)} %param.13) | copy-start | bytes 52
  57.1 33.7 %copy-start.4 = (f32[128,256]{1,0:T(8,128)S(1)}, f32[128,256]{1,0:T(8,128)}, u32[]{:S(2)}) copy-start(f32[128,256]{1,0:T(8,128)} %param.8) | copy-start | bytes 393220
  98.5 5.0 copy-start.14
  101.8 0.6 copy-start.18
  107.1 4.9 copy-start.7
  112.1 33.6 %copy-start.3 = (s32[1,1,6,128,128]{4,3,2,1,0:T(8,128)S(1)}, s32[1,1,6,128,128]{4,3,2,1,0:T(8,128)}, u32[]{:S(2)}) copy-start(s32[1,1,6,128,128]{4,3,2,1,0:T(8,128)} %get-tuple-element.4) | copy-start | bytes 1179652
  112.1 34.4 %copy-start.10 = (s32[6]{0:T(128)S(1)}, s32[6]{0:T(128)}, u32[]{:S(2)}) copy-start(s32[6]{0:T(128)} %get-tuple-element.11) | copy-start | bytes 76
  145.3 7.6 collective-permute-start
  198.4 33.6 %copy-start.19 = (bf16[128,256]{1,0:T(8,128)(2,1)S(1)}, bf16[128,256]{1,0:T(8,128)(2,1)}, u32[]{:S(2)}) copy-start(bf16[128,256]{1,0:T(8,128)(2,1)} %copy-done.18) | copy-start | bytes 196612
  235.1 4.9 copy-start.13
  248.7 34.4 %copy-start.9 = (s32[6]{0:T(128)S(1)}, s32[6]{0:T(128)}, u32[]{:S(2)}) copy-start(s32[6]{0:T(128)} %get-tuple-element.13) | copy-start | bytes 76
  281.8 93.2 %collective-permute-start.1 = (f32[4096,256]{1,0:T(8,128)}, f32[4096,256]{1,0:T(8,128)}, u32[]{:S(2)}, u32[]{:S(2)}) collective-permute-start(f32[4096,256]{1,0:T(8,128)} %add_multiply_fusion.2), channel_id=1, source_target_pairs={{0,16},{8,24},{16,0},{24,8},{32,48},{40,56},{48,32},{56,40},{64,80... | collective-permute-start | bytes 12582920 | tf_op jit(solution)/shard_map/ppermute | solution.py:22
  416.0 33.2 %copy-start.17 = (bf16[128,256]{1,0:T(8,128)(2,1)S(1)}, bf16[128,256]{1,0:T(8,128)(2,1)}, u32[]{:S(2)}) copy-start(bf16[128,256]{1,0:T(8,128)(2,1)} %copy-done.16) | copy-start | bytes 196612
  452.3 4.3 copy-start.12
  465.2 34.6 %copy-start.8 = (s32[6]{0:T(128)S(1)}, s32[6]{0:T(128)}, u32[]{:S(2)}) copy-start(s32[6]{0:T(128)} %get-tuple-element.10) | copy-start | bytes 76
  498.4 7.8 collective-permute-start.2
  587.0 2.3 copy-start.15
  587.0 2.7 copy-start.11
  598.4 251.6 %copy-start.1 = (f32[1024,256]{1,0:T(8,128)S(1)}, f32[1024,256]{1,0:T(8,128)}, u32[]{:S(2)}) copy-start(f32[1024,256]{1,0:T(8,128)} %param.9) | copy-start | bytes 3145732
  629.8 93.0 %collective-permute-start.3 = (f32[4096,256]{1,0:T(8,128)S(1)}, f32[4096,256]{1,0:T(8,128)}, u32[]{:S(2)}, u32[]{:S(2)}) collective-permute-start(f32[4096,256]{1,0:T(8,128)S(1)} %add_multiply_fusion), channel_id=1, source_target_pairs={{0,16},{8,24},{16,0},{24,8},{32,48},{40,56},{48,32},{56,40},{64,80... | collective-permute-start | bytes 12582920 | tf_op jit(solution)/shard_map/ppermute | solution.py:22
  (1 other events, 0.6 us)
Sparse Core Ops, SparseCore 0:
  722.9 125.2 reduce-scatter.1
